TPU v7x, 32 devices: a whole 2x2x4 slice. The times are simulated.
32 devices in a mesh: row: 2 (over x), feat: 16 (over z, y, core).
Axes of the slice: x: 2, y: 2, z: 4, core: 2. Of those that a mesh axis runs over, the one named last changes fastest.
Arguments:
- logits: bfloat16 [2048, 1000], P(('row', 'feat')), may hold values from -200 to 200, as said below
- labels: int32 [2048], P(('row', 'feat')), may hold values from 0 to 999
- projection: bfloat16 [1000, 16], replicated, may hold values from -4 to 4
- bins: int32 [2048, 2048], P('feat', 'row'), may hold values from 0 to 63, as said below
- nbins: int32 [2048], P('feat'), may hold values from 2 to 64
- leaf: int32 [2048], P('row'), may hold values from 0 to 15
Outputs:
- relative_gain: float32 [16, 131072], P('row', 'feat')
Inputs may be any that keep to these rules, and one draw needn't show every extreme that they name: `logits`: shows the class scores; some rows may lie far from zero. bins[f, i] < nbins[f].
All inputs are finite; a program needn't handle non-finite values.
Results may differ from a plain program's by a relative error of at most 0.0017.
Values may be sent and summed in bfloat16 or wider, within the bound.
No kernel may reach another device: no remote copies, remote signals or barrier semaphores. Data moves between devices by JAX's collectives and lax.ppermute only.
A program may use at most 64 MiB of HBM per device.

v0:
```python
import functools

import jax
import jax.numpy as jnp
from jax import lax
from jax.experimental import pallas as pl
from jax.experimental.pallas import tpu as pltpu
from jax.sharding import PartitionSpec as P


BINS = 64
LEAVES = 16
LANES = 128
UNROLLED = 1 << 24
HALF = 36
PARTS = 4
QUARTER = 48
GRANT = 16 << 20
ridge = 1.0
epsilon = 1e-06


def vmem():
    return pl.BlockSpec(memory_space=pltpu.VMEM)


def lanes_of(features):
    return features * max(1, LANES // features)


def prepare_kernel(*refs):
    bins_hbm, leaf_hbm, logits_hbm, labels_hbm, projection_hbm, nbins_hbm, turned_ref, values_ref, nbins_ref = refs[:9]
    bins_ref, leaf_ref, logits_ref, labels_ref, projection_ref, arrived = refs[9:]
    pairs = (
        (logits_hbm, logits_ref),
        (labels_hbm, labels_ref),
        (projection_hbm, projection_ref),
        (bins_hbm, bins_ref),
        (leaf_hbm, leaf_ref),
        (nbins_hbm, nbins_ref),
    )
    arrivals = [pltpu.make_async_copy(a, b, arrived.at[i]) for i, (a, b) in enumerate(pairs)]
    for arrival in arrivals:
        arrival.start()
    for arrival in arrivals[:3]:
        arrival.wait()

    rows, classes = logits_ref.shape
    scores = logits_ref[...].astype(jnp.float32)
    highest = jnp.max(scores, axis=1, keepdims=True)
    expd = jnp.exp(scores - highest)
    probability = expd / jnp.sum(expd, axis=1, keepdims=True)
    labels = jnp.broadcast_to(labels_ref[...].astype(jnp.float32), (LANES, rows))
    labels = jnp.transpose(labels)[:, :1].astype(jnp.int32)
    lane = lax.broadcasted_iota(jnp.int32, (rows, classes), 1)
    target = jnp.where(lane == labels, 1.0, 0.0)
    gradient = (probability - target).astype(jnp.bfloat16)
    sketch = lax.dot_general(
        projection_ref[...], gradient, (((1,), (1,)), ((), ())), preferred_element_type=jnp.float32
    )
    hessian = jnp.sum(probability * (1.0 - probability), axis=1, keepdims=True)
    hessian = jnp.transpose(jnp.broadcast_to(hessian, (rows, LANES)))[:1, :]
    top = sketch[:10]
    low = jnp.concatenate([sketch[10:], hessian, jnp.zeros((3, rows), jnp.float32)], axis=0)
    packed = jnp.concatenate([top, low], axis=1)
    odd = lax.rem(lax.axis_index("feat"), 2)
    packed = jnp.where(odd == 1, pltpu.roll(packed, rows, 1), packed).astype(jnp.bfloat16)
    for c in range(5):
        block = packed[2 * c : 2 * c + 2]
        cols = slice(c * LANES, (c + 1) * LANES)
        values_ref[:, :, cols] = jnp.broadcast_to(block[None], (values_ref.shape[0], 2, LANES))

    for arrival in arrivals[3:]:
        arrival.wait()
    lines = bins_ref.shape[1]
    turned = jnp.transpose(bins_ref[...].astype(jnp.float32))
    copies = turned_ref.shape[1] // bins_ref.shape[0]
    if copies > 1:
        turned = jnp.concatenate([turned] * copies, axis=1)
    turned_ref[:lines, :] = turned.astype(jnp.bfloat16)
    leaf = leaf_ref[...].astype(jnp.float32)
    spare = turned_ref.shape[0] - lines - leaf.shape[0]
    leaf = jnp.concatenate([leaf, jnp.zeros((spare, LANES), jnp.float32)], axis=0) if spare else leaf
    turned_ref[lines:, :LANES] = leaf.astype(jnp.bfloat16)


def prepare(bins, leaf, logits, labels, projection, nbins, destinations):
    features, lines = bins.shape
    rows = logits.shape[0]
    tail = -(-lines // LANES // 16) * 16
    width = lanes_of(features)
    counts = jnp.tile(nbins, width // features).reshape(1, width)
    given = (bins, leaf.reshape(lines // LANES, LANES), logits, labels.reshape(1, rows), projection.T, counts)
    return pl.pallas_call(
        prepare_kernel,
        out_shape=(
            jax.ShapeDtypeStruct((lines + tail, lanes_of(features)), jnp.bfloat16),
            jax.ShapeDtypeStruct((destinations, 2, 10 * rows), jnp.bfloat16),
            jax.ShapeDtypeStruct((1, width), jnp.int32),
        ),
        in_specs=[pl.BlockSpec(memory_space=pltpu.HBM)] * 6,
        out_specs=(vmem(), vmem(), vmem()),
        scratch_shapes=[pltpu.VMEM(x.shape, x.dtype) for x in given[:5]] + [pltpu.SemaphoreType.DMA((6,))],
        compiler_params=pltpu.CompilerParams(vmem_limit_bytes=16 << 20),
        name="prepare",
    )(*[pltpu.with_memory_space_constraint(x, pltpu.HBM) for x in given])


def padded(share):
    return -(-17 * share // 16) * 16


def fill_weights(share, shard, values_ref, bins_ref, weights, table):
    sources, half = values_ref.shape[0] // lax.axis_size("row"), LANES // 2
    rows = sources * half
    wide = (share, LANES)
    my_leaf = lax.broadcasted_iota(jnp.int32, wide, 0) + lax.axis_index("row") * share
    my_leaf = my_leaf.astype(jnp.float32)
    left_half = lax.broadcasted_iota(jnp.int32, (2, LANES), 1) < half
    for pair in range(sources // 2):
        columns = [None] * 20
        for c in range(5):
            cols = slice(c * LANES, (c + 1) * LANES)
            first = values_ref[shard * sources + 2 * pair, :, cols].astype(jnp.float32)
            second = values_ref[shard * sources + 2 * pair + 1, :, cols].astype(jnp.float32)
            top = jnp.where(left_half, first, second)
            low = pltpu.roll(jnp.where(left_half, second, first), half, 1)
            columns[2 * c : 2 * c + 2] = top[:1], top[1:]
            columns[10 + 2 * c : 12 + 2 * c] = low[:1], low[1:]
        at = rows + pair // 16 * 16
        leaf = bins_ref[at : at + 16, :LANES].astype(jnp.float32)[pair % 16 : pair % 16 + 1]
        mine = jnp.broadcast_to(leaf, wide) == my_leaf
        pieces = []
        for k in range(17):
            piece = jnp.where(mine, jnp.broadcast_to(columns[k], wide), 0.0)
            pieces.append(piece)
        spare = padded(share) - 17 * share
        if spare:
            pieces.append(jnp.zeros((spare, LANES), jnp.float32))
        lines = jnp.concatenate(pieces, axis=0).astype(jnp.bfloat16)
        weights[:, pair * LANES : (pair + 1) * LANES] = lines
    table[...] = bins_ref[:rows, :].astype(jnp.float32)


def left_sums(ids, weights, tables):
    one, zero = jnp.bfloat16(1.0), jnp.bfloat16(0.0)
    bins = {id(ref): ref[...].astype(jnp.bfloat16) for ref in tables}
    ids = [i.astype(jnp.float32).astype(jnp.bfloat16) for i in ids]
    hot = [jnp.where(bins[id(ref)] <= i, one, zero) for i, ref in zip(ids, tables)]
    return jnp.dot(weights[...], jnp.concatenate(hot, axis=1), preferred_element_type=jnp.float32)


def gain_kernel(share, features, steps, values_ref, nbins_ref, *refs):
    n_row = lax.axis_size("row")
    bins_refs, (gain_ref, best_ref, weights, table, most_ref) = refs[:n_row], refs[n_row : n_row + 5]
    sorted_refs = refs[n_row + 5 :]
    rows, width = table.shape[0] // n_row, table.shape[1]
    full = (share, width)
    for s in range(n_row):
        shard = lax.rem(lax.axis_index("row") + s, n_row)
        these = pl.ds(s * rows, rows)
        fill_weights(share, shard, values_ref, bins_refs[s], weights.at[:, these], table.at[these, :])

    def score(sums):
        squares = sums[0] * sums[0]
        for k in range(1, 16):
            squares = squares + sums[k] * sums[k]
        return squares / (sums[16] + ridge)

    copies = width // features
    bin_of = lax.broadcasted_iota(jnp.int32, (1, width), 1) // features
    last = jnp.broadcast_to(nbins_ref[...] - 1, full)

    def gain_of(sums, j, totals, of_all):
        left = [sums[k * share : (k + 1) * share, j * width : (j + 1) * width] for k in range(17)]
        right = [totals[k] - left[k] for k in range(17)]
        return score(left) + score(right) - of_all

    def keep(at, ids, gain, best):
        gain = jnp.where(jnp.broadcast_to(ids, full) < last, gain, 0.0)
        gain_ref[at] = gain
        return jnp.maximum(best, gain)

    def add_group(totals, of_all, g, best):
        ids = [bin_of + (g * steps + j) * copies for j in range(steps)]
        sums = left_sums(ids, weights, [table] * steps)
        for j in range(steps):
            best = keep(g * steps + j, ids[j], gain_of(sums, j, totals, of_all), best)
        return best

    lowest = jnp.full(full, -jnp.inf, jnp.float32)

    def every_feature():
        totals = []
        for k in range(17):
            line = weights[k * share : (k + 1) * share, :].astype(jnp.float32)
            totals.append(jnp.broadcast_to(jnp.sum(line, axis=1, keepdims=True), full))
        add = functools.partial(add_group, totals, score(totals))
        most_ref[...] = lax.fori_loop(0, BINS // copies // steps, add, lowest)

    if not sorted_refs:
        every_feature()
    else:
        halves, quarters = sorted_refs
        square = (LANES, LANES)
        counts = jnp.broadcast_to(nbins_ref[...].astype(jnp.float32), square)
        other = jnp.transpose(counts)
        index = lax.broadcasted_iota(jnp.int32, square, 0)
        lane = lax.broadcasted_iota(jnp.int32, square, 1)
        ahead = jnp.where(other > counts, 1.0, jnp.where((other == counts) & (index < lane), 1.0, 0.0))
        rank = jnp.sum(ahead, axis=0, keepdims=True)
        turned = jnp.transpose(jnp.broadcast_to(rank, square)).astype(jnp.int32)
        rank = jnp.broadcast_to(rank.astype(jnp.int32), full)
        few = (last[:1] > HALF) & (rank[:1] >= LANES // 2) | (last[:1] > QUARTER) & (rank[:1] >= LANES // 4)
        fits = jnp.sum(jnp.where(few, 1, 0)) == 0

        @pl.when(fits)
        def _():
            bins = table[...].astype(jnp.bfloat16)
            for part, ref in ((2, halves), (4, quarters)):
                pick = jnp.where(turned == lax.rem(lane, LANES // part), 1.0, 0.0).astype(jnp.bfloat16)
                ref[...] = jnp.dot(bins, pick, preferred_element_type=jnp.float32)
            tiles = [(b, 4, quarters) for b in range(BINS - 4, QUARTER - 1, -4)]
            tiles += [(b, 2, halves) for b in range(HALF, QUARTER, 2)]
            tiles += [(b, 1, table) for b in range(HALF)]
            lanes = lax.broadcasted_iota(jnp.int32, (1, LANES), 1)
            ids = [b + lanes // (LANES // part) for b, part, _ in tiles]
            sums = left_sums(ids, weights, [ref for _, _, ref in tiles])
            best = lowest
            every = [sums[k * share : (k + 1) * share, LANES - 1 : LANES] for k in range(17)]
            totals = [jnp.broadcast_to(t, full) for t in every]
            of_all = score(totals)
            for j, (b, part, _) in enumerate(tiles):
                gain = gain_of(sums, j, totals, of_all)
                for sub in range(part):
                    own = gain
                    if part > 1:
                        at = jnp.minimum(rank + sub * (LANES // part), LANES - 1)
                        own = jnp.take_along_axis(gain, at, axis=1, mode="promise_in_bounds")
                    best = keep(b + sub, jnp.full((1, LANES), b + sub, jnp.int32), own, best)
            most_ref[...] = best

        pl.when(jnp.logical_not(fits))(every_feature)

    best = most_ref[...]
    best = jnp.broadcast_to(jnp.max(best, axis=1, keepdims=True), (share, LANES))
    mine = lax.broadcasted_iota(jnp.int32, (share, LANES), 0) == lax.broadcasted_iota(jnp.int32, (share, LANES), 1)
    best = jnp.max(jnp.where(mine, best, -jnp.inf), axis=0, keepdims=True)
    best_ref[...] = jnp.broadcast_to(best[None], best_ref.shape)


def split_gains(values, counts, bins, share, features, destinations):
    width = bins[0].shape[1]
    copies = width // features
    rows = values.shape[0] * LANES // 2
    steps = BINS // copies
    while steps % 2 == 0 and rows * width * steps > UNROLLED:
        steps //= 2
    held = rows * (4 * width + 2 * padded(share))
    sort = features == LANES and steps == BINS
    return pl.pallas_call(
        functools.partial(gain_kernel, share, features, steps),
        out_shape=(
            jax.ShapeDtypeStruct((BINS // copies, share, width), jnp.float32),
            jax.ShapeDtypeStruct((destinations, 1, LANES), jnp.float32),
        ),
        in_specs=[vmem()] * (2 + len(bins)),
        out_specs=(vmem(), vmem()),
        scratch_shapes=[
            pltpu.VMEM((padded(share), rows), jnp.bfloat16),
            pltpu.VMEM((rows, width), jnp.float32),
            pltpu.VMEM((share, width), jnp.float32),
        ]
        + [pltpu.VMEM((rows, width), jnp.float32)] * (2 if sort else 0),
        compiler_params=pltpu.CompilerParams(vmem_limit_bytes=GRANT + 2 * held),
        name="gains",
    )(values, counts, *bins)


def finish_kernel(gain_ref, best_ref, out_hbm, turned, lines, staged, sems):
    share, features = out_hbm.shape[0], turned.shape[1]
    half = features // 2
    wide = (share, LANES)
    best = jnp.broadcast_to(jnp.max(best_ref[...], axis=0), wide)
    mine = lax.broadcasted_iota(jnp.int32, wide, 0) == lax.broadcasted_iota(jnp.int32, wide, 1)
    best = jnp.max(jnp.where(mine, best, -jnp.inf), axis=1, keepdims=True)
    divisor = jnp.broadcast_to(best + epsilon, wide)
    first = lax.broadcasted_iota(jnp.int32, (half, LANES), 1) < BINS
    for leaf in range(0, share, 2):
        both = [gain_ref[pl.ds(leaf + one, BINS, stride=share), :] for one in range(2)]
        turned[leaf // 2] = jnp.transpose(jnp.concatenate(both, axis=0))
        even, odd = (turned[leaf // 2, pl.ds(start, half, stride=2), :] for start in range(2))
        lines[pl.ds(leaf, half, stride=share), :] = jnp.where(first, even, pltpu.roll(odd, BINS, 1))
        lines[pl.ds(leaf + 1, half, stride=share), :] = jnp.where(first, pltpu.roll(even, BINS, 1), odd)
    copies = []
    for part in range(PARTS):
        for j in range(part * half // PARTS, (part + 1) * half // PARTS):
            staged[:, j * LANES : (j + 1) * LANES] = lines[j * share : (j + 1) * share, :] / divisor
        cols = pl.ds(part * half // PARTS * LANES, half // PARTS * LANES)
        copies.append(pltpu.make_async_copy(staged.at[:, cols], out_hbm.at[:, cols], sems.at[part]))
        copies[-1].start()
    for copy in copies:
        copy.wait()


def finish(gain, best, features):
    share = gain.shape[1]
    return pl.pallas_call(
        finish_kernel,
        out_shape=jax.ShapeDtypeStruct((share, features * BINS), jnp.float32),
        in_specs=[vmem(), vmem()],
        out_specs=pl.BlockSpec(memory_space=pltpu.HBM),
        scratch_shapes=[
            pltpu.VMEM((share // 2, features, LANES), jnp.float32),
            pltpu.VMEM((features // 2 * share, LANES), jnp.float32),
            pltpu.VMEM((share, features * BINS), jnp.float32),
            pltpu.SemaphoreType.DMA((PARTS,)),
        ],
        compiler_params=pltpu.CompilerParams(vmem_limit_bytes=GRANT),
        name="finish",
    )(gain.reshape(BINS * share, features), best)


def on_device(n_row, n_feat, logits, labels, projection, bins, nbins, leaf):
    own, copies, counts = prepare(bins, leaf, logits, labels, projection, nbins, n_row * n_feat)
    values = lax.all_to_all(copies, ("row", "feat"), 0, 0)
    all_bins = [own]
    for s in range(1, n_row):
        all_bins.append(lax.ppermute(own, "row", [((i + s) % n_row, i) for i in range(n_row)]))
    share, features = LEAVES // n_row, bins.shape[0]
    gain, best = split_gains(values, counts, all_bins, share, features, n_feat)
    if features == LANES == 2 * BINS and share % 8 == 0:
        return finish(gain, lax.all_to_all(best, "feat", 0, 0), features)
    gain = gain.transpose(1, 0, 2).reshape(share, BINS, features).transpose(0, 2, 1)
    gain, best = lax.optimization_barrier((gain.reshape(share, features * BINS), best))
    best = lax.all_to_all(best, "feat", 0, 0)
    return gain / (jnp.max(best, axis=(0, 1))[:share, None] + epsilon)


def solution(mesh):
    return jax.shard_map(
        functools.partial(on_device, mesh.shape["row"], mesh.shape["feat"]),
        mesh=mesh,
        in_specs=(
            P(("row", "feat"), None),
            P(("row", "feat")),
            P(),
            P("feat", "row"),
            P("feat"),
            P("row"),
        ),
        out_specs=P("row", "feat"),
        check_vma=False,
    )
```

profile of v0, /device:TPU:0, one launch (start us, length us, event | category | flops | bytes accessed | tf_op | source)
XLA Modules:
  0.0 31.5 jit_solution(5336548537259304458)
XLA Ops:
  0.0 1.7 %prepare.1 = (bf16[1040,128]{1,0:T(8,128)(2,1)S(1)}, bf16[32,2,640]{2,1,0:T(2,128)(2,1)S(1)}, s32[1,128]{1,0:T(1,128)S(1)}) custom-call(s32[128,1024]{1,0:T(8,128)} %refs_0_.1, s32[8,128]{1,0:T(8,128)} %bitcast.7, bf16[64,1000]{1,0:T(8,128)(2,1)} %refs_2_.1, s32[1,64]{1,0:T(1,128)} %bitcast.8, bf16[16,1000]{1,0:T(8,128)(2,1)} %bitcast.6, s32[1,128]{1,0:T(1,128)} %bitcast.9), custom_call_target="tpu_custom_call" | custom-call | tf_op jit(solution)/shard_map/prepare/pallas_call | solution.py:94
  1.7 3.0 %collective-permute-start = (bf16[1040,128]{1,0:T(8,128)(2,1)S(1)}, bf16[1040,128]{1,0:T(8,128)(2,1)S(1)}, u32[]{:S(2)}, u32[]{:S(2)}) collective-permute-start(bf16[1040,128]{1,0:T(8,128)(2,1)S(1)} %get-tuple-element.12.refs_0_), channel_id=1, source_target_pairs={{16,0},{0,16},{17,1},{1,17},{18,2},{2,18},{19,3},{3,19},{20,4},{4,... | collective-permute-start | bytes 798728 | tf_op jit(solution)/shard_map/ppermute | solution.py:329
  4.7 12.3 %all_to_all.10.values_ref = bf16[32,2,640]{2,1,0:T(2,128)(2,1)S(1)} all-to-all(bf16[32,2,640]{2,1,0:T(2,128)(2,1)S(1)} %get-tuple-element.10), channel_id=1, replica_groups=mesh['row'=2,'feat'=16] {'row','feat'}, dimensions={0} | all-to-all | bytes 163840 | tf_op jit(solution)/shard_map/all_to_all | solution.py:326
  17.0 0.0 collective-permute-done.refs_1_
  17.0 4.5 %gains.1 = (f32[64,8,128]{2,1,0:T(8,128)S(1)}, f32[16,1,128]{2,1,0:T(1,128)S(1)}) custom-call(bf16[32,2,640]{2,1,0:T(2,128)(2,1)S(1)} %all_to_all.10.values_ref, s32[1,128]{1,0:T(1,128)S(1)} %get-tuple-element.11.nbins_ref, bf16[1040,128]{1,0:T(8,128)(2,1)S(1)} %get-tuple-element.12.refs_0_, bf16[1040,128]{1,0:T(8,128)(2,1)S(1)} %collective-permute-done.refs_1_), custom_call_target="tpu_custom_call" | custom-call | tf_op jit(solution)/shard_map/gains/pallas_call | solution.py:261
  21.6 9.0 %all_to_all.11.best_ref = f32[16,1,128]{2,1,0:T(1,128)S(1)} all-to-all(f32[16,1,128]{2,1,0:T(1,128)S(1)} %get-tuple-element.14), channel_id=1, replica_groups=mesh['row'=2,'feat'=16] {'feat'}, dimensions={0} | all-to-all | bytes 16384 | tf_op jit(solution)/shard_map/all_to_all | solution.py:333
  30.6 1.0 %finish.1 = f32[8,8192]{1,0:T(8,128)} custom-call(f32[512,128]{1,0:T(8,128)S(1)} %bitcast.5, f32[16,1,128]{2,1,0:T(1,128)S(1)} %all_to_all.11.best_ref), custom_call_target="tpu_custom_call" | custom-call | tf_op jit(solution)/shard_map/finish/pallas_call | solution.py:308
Async XLA Ops:
  1.7 15.3 %collective-permute-start = (bf16[1040,128]{1,0:T(8,128)(2,1)S(1)}, bf16[1040,128]{1,0:T(8,128)(2,1)S(1)}, u32[]{:S(2)}, u32[]{:S(2)}) collective-permute-start(bf16[1040,128]{1,0:T(8,128)(2,1)S(1)} %get-tuple-element.12.refs_0_), channel_id=1, source_target_pairs={{16,0},{0,16},{17,1},{1,17},{18,2},{2,18},{19,3},{3,19},{20,4},{4,... | collective-permute-start | bytes 798728 | tf_op jit(solution)/shard_map/ppermute | solution.py:329
where the time goes:
time: 31.7 us; the launch traced here: 31.5 us
  blocking collectives  21.3 us (67%)
  Pallas kernels  7.2 us (23%)
  starting transfers between devices  3.03 us (10%)
    all_to_all x1, blocking collectives, on_device(): values = lax.all_to_all(copies, ('row', 'feat'), 0, 0)  12.3 us
    all_to_all x1, blocking collectives, on_device(): return finish(gain, lax.all_to_all(best, 'feat', 0, 0), features)  9 us
    pallas_call x1, Pallas kernels, split_gains(): pl.pallas_call(functools.partial(gain_kernel, share, features, steps), ou...  4.52 us
    ppermute x1, starting transfers between devices, on_device(): lax.ppermute(own, 'row', [((i + s) % n_row, i) for i in range(n_row)])  3.03 us
    pallas_call x1, Pallas kernels, prepare(): pl.pallas_call(prepare_kernel, out_shape=(jax.ShapeDtypeStruct((lines + t...  1.69 us
    pallas_call x1, Pallas kernels, finish(): pl.pallas_call(finish_kernel, out_shape=jax.ShapeDtypeStruct((share, feat...  0.98 us
  transfers between devices with their start and end apart: 1, of which 0 were waited for; matrix products, arithmetic and copies ran while one was open for 0% of the time, Pallas kernels for 0%

commit v1 on v0

--- a/solution.py
+++ b/solution.py
@@ -12,9 +12,9 @@
 LEAVES = 16
 LANES = 128
 UNROLLED = 1 << 24
-HALF = 36
+HALF = 38
 PARTS = 4
-QUARTER = 48
+QUARTER = 52
 GRANT = 16 << 20
 ridge = 1.0
 epsilon = 1e-06
@@ -49,6 +49,8 @@
     scores = logits_ref[...].astype(jnp.float32)
     highest = jnp.max(scores, axis=1, keepdims=True)
     expd = jnp.exp(scores - highest)
+    for arrival in arrivals[3:]:
+        arrival.wait()
     probability = expd / jnp.sum(expd, axis=1, keepdims=True)
     labels = jnp.broadcast_to(labels_ref[...].astype(jnp.float32), (LANES, rows))
     labels = jnp.transpose(labels)[:, :1].astype(jnp.int32)
@@ -70,8 +72,6 @@
         cols = slice(c * LANES, (c + 1) * LANES)
         values_ref[:, :, cols] = jnp.broadcast_to(block[None], (values_ref.shape[0], 2, LANES))
 
-    for arrival in arrivals[3:]:
-        arrival.wait()
     lines = bins_ref.shape[1]
     turned = jnp.transpose(bins_ref[...].astype(jnp.float32))
     copies = turned_ref.shape[1] // bins_ref.shape[0]
@@ -216,10 +216,13 @@
 
         @pl.when(fits)
         def _():
-            bins = table[...].astype(jnp.bfloat16)
-            for part, ref in ((2, halves), (4, quarters)):
-                pick = jnp.where(turned == lax.rem(lane, LANES // part), 1.0, 0.0).astype(jnp.bfloat16)
-                ref[...] = jnp.dot(bins, pick, preferred_element_type=jnp.float32)
+            picks = [jnp.where(turned == lax.rem(lane, LANES // part), 1.0, 0.0) for part in (2, 4)]
+            picks = jnp.concatenate(picks, axis=1).astype(jnp.bfloat16)
+            for s in range(n_row):
+                these = slice(s * rows, (s + 1) * rows)
+                bins = table[these, :].astype(jnp.bfloat16)
+                picked = jnp.dot(bins, picks, preferred_element_type=jnp.float32)
+                halves[these, :], quarters[these, :] = picked[:, :LANES], picked[:, LANES:]
             tiles = [(b, 4, quarters) for b in range(BINS - 4, QUARTER - 1, -4)]
             tiles += [(b, 2, halves) for b in range(HALF, QUARTER, 2)]
             tiles += [(b, 1, table) for b in range(HALF)]

time: 31.7 us -> 31.8 us (level)
  no operation moved by 1% of the time
where the time goes in v1:
time: 31.8 us; the launch traced here: 31.6 us
  blocking collectives  21.3 us (67%)
  Pallas kernels  7.29 us (23%)
  starting transfers between devices  3.03 us (10%)
    all_to_all x1, blocking collectives, on_device(): values = lax.all_to_all(copies, ('row', 'feat'), 0, 0)  12.3 us
    all_to_all x1, blocking collectives, on_device(): return finish(gain, lax.all_to_all(best, 'feat', 0, 0), features)  9 us
    pallas_call x1, Pallas kernels, split_gains(): pl.pallas_call(functools.partial(gain_kernel, share, features, steps), ou...  4.58 us
    ppermute x1, starting transfers between devices, on_device(): lax.ppermute(own, 'row', [((i + s) % n_row, i) for i in range(n_row)])  3.03 us
    pallas_call x1, Pallas kernels, prepare(): pl.pallas_call(prepare_kernel, out_shape=(jax.ShapeDtypeStruct((lines + t...  1.73 us
    pallas_call x1, Pallas kernels, finish(): pl.pallas_call(finish_kernel, out_shape=jax.ShapeDtypeStruct((share, feat...  0.98 us
  transfers between devices with their start and end apart: 1, of which 0 were waited for; matrix products, arithmetic and copies ran while one was open for 0% of the time, Pallas kernels for 0%

profile of v1, /device:TPU:0, one launch (start us, length us, event | category | flops | bytes accessed | tf_op | source)
XLA Modules:
  0.0 31.6 jit_solution(8895200966241454491)
XLA Ops:
  0.0 1.7 %prepare.1 = (bf16[1040,128]{1,0:T(8,128)(2,1)S(1)}, bf16[32,2,640]{2,1,0:T(2,128)(2,1)S(1)}, s32[1,128]{1,0:T(1,128)S(1)}) custom-call(s32[128,1024]{1,0:T(8,128)} %refs_0_.1, s32[8,128]{1,0:T(8,128)} %bitcast.7, bf16[64,1000]{1,0:T(8,128)(2,1)} %refs_2_.1, s32[1,64]{1,0:T(1,128)} %bitcast.8, bf16[16,1000]{1,0:T(8,128)(2,1)} %bitcast.6, s32[1,128]{1,0:T(1,128)} %bitcast.9), custom_call_target="tpu_custom_call" | custom-call | tf_op jit(solution)/shard_map/prepare/pallas_call | solution.py:94
  1.7 3.0 %collective-permute-start = (bf16[1040,128]{1,0:T(8,128)(2,1)S(1)}, bf16[1040,128]{1,0:T(8,128)(2,1)S(1)}, u32[]{:S(2)}, u32[]{:S(2)}) collective-permute-start(bf16[1040,128]{1,0:T(8,128)(2,1)S(1)} %get-tuple-element.12.refs_0_), channel_id=1, source_target_pairs={{16,0},{0,16},{17,1},{1,17},{18,2},{2,18},{19,3},{3,19},{20,4},{4,... | collective-permute-start | bytes 798728 | tf_op jit(solution)/shard_map/ppermute | solution.py:332
  4.8 12.3 %all_to_all.10.values_ref = bf16[32,2,640]{2,1,0:T(2,128)(2,1)S(1)} all-to-all(bf16[32,2,640]{2,1,0:T(2,128)(2,1)S(1)} %get-tuple-element.10), channel_id=1, replica_groups=mesh['row'=2,'feat'=16] {'row','feat'}, dimensions={0} | all-to-all | bytes 163840 | tf_op jit(solution)/shard_map/all_to_all | solution.py:329
  17.1 0.0 collective-permute-done.refs_1_
  17.1 4.6 %gains.1 = (f32[64,8,128]{2,1,0:T(8,128)S(1)}, f32[16,1,128]{2,1,0:T(1,128)S(1)}) custom-call(bf16[32,2,640]{2,1,0:T(2,128)(2,1)S(1)} %all_to_all.10.values_ref, s32[1,128]{1,0:T(1,128)S(1)} %get-tuple-element.11.nbins_ref, bf16[1040,128]{1,0:T(8,128)(2,1)S(1)} %get-tuple-element.12.refs_0_, bf16[1040,128]{1,0:T(8,128)(2,1)S(1)} %collective-permute-done.refs_1_), custom_call_target="tpu_custom_call" | custom-call | tf_op jit(solution)/shard_map/gains/pallas_call | solution.py:264
  21.7 9.0 %all_to_all.11.best_ref = f32[16,1,128]{2,1,0:T(1,128)S(1)} all-to-all(f32[16,1,128]{2,1,0:T(1,128)S(1)} %get-tuple-element.14), channel_id=1, replica_groups=mesh['row'=2,'feat'=16] {'feat'}, dimensions={0} | all-to-all | bytes 16384 | tf_op jit(solution)/shard_map/all_to_all | solution.py:336
  30.7 1.0 %finish.1 = f32[8,8192]{1,0:T(8,128)} custom-call(f32[512,128]{1,0:T(8,128)S(1)} %bitcast.5, f32[16,1,128]{2,1,0:T(1,128)S(1)} %all_to_all.11.best_ref), custom_call_target="tpu_custom_call" | custom-call | tf_op jit(solution)/shard_map/finish/pallas_call | solution.py:311
Async XLA Ops:
  1.7 15.3 %collective-permute-start = (bf16[1040,128]{1,0:T(8,128)(2,1)S(1)}, bf16[1040,128]{1,0:T(8,128)(2,1)S(1)}, u32[]{:S(2)}, u32[]{:S(2)}) collective-permute-start(bf16[1040,128]{1,0:T(8,128)(2,1)S(1)} %get-tuple-element.12.refs_0_), channel_id=1, source_target_pairs={{16,0},{0,16},{17,1},{1,17},{18,2},{2,18},{19,3},{3,19},{20,4},{4,... | collective-permute-start | bytes 798728 | tf_op jit(solution)/shard_map/ppermute | solution.py:332
